TPU v7x, 32 devices: a whole 2x2x4 slice. The times are simulated.
32 devices in a mesh: dap: 8 (over z, core), ch: 4 (over y, x).
Axes of the slice: x: 2, y: 2, z: 4, core: 2. Of those that a mesh axis runs over, the one named last changes fastest.
Arguments:
- pair_rep: bfloat16 [120, 120, 128], P('dap', 'ch'), may hold values from -400 to 400
- residue_mask: int32 [120], replicated, may hold values 0 or 1
- w_proj: bfloat16 [128, 512], replicated, may hold values from -0.5 to 0.5
- w_gate: bfloat16 [128, 128], replicated, may hold values from -0.5 to 0.5
- w_out: bfloat16 [128, 128], replicated, may hold values from -0.5 to 0.5
- cotangent: bfloat16 [120, 120, 128], P('dap', 'ch'), may hold values from -6 to 6
Outputs:
- pair_update: bfloat16 [120, 120, 128], P('dap', 'ch')
- grad_pair: bfloat16 [120, 120, 128], P('dap', 'ch')
Inputs may be any that keep to these rules, and one draw needn't show every extreme that they name: `residue_mask`: 1 marks a residue of the crop, 0 a padding position.
All inputs are finite; a program needn't handle non-finite values.
Results may differ from a plain program's by a relative error of at most 0.0085.
Values may be sent and summed in bfloat16 or wider, within the bound.
No kernel may reach another device: no remote copies, remote signals or barrier semaphores. Data moves between devices by JAX's collectives and lax.ppermute only.
A program may use at most 64 MiB of HBM per device.

v0:
```python
import jax
import jax.numpy as jnp
from jax import lax
from jax.sharding import PartitionSpec as P

EPSILON = 1e-05


def normalize(values, axis):
    center = jnp.mean(values, axis=axis, keepdims=True)
    spread = values - center
    scale_inv = lax.rsqrt(jnp.mean(spread * spread, axis=axis, keepdims=True) + EPSILON)
    return (spread * scale_inv, scale_inv)


def norm_back(grad_in, normed, scale_inv, axis):
    first = jnp.mean(grad_in, axis=axis, keepdims=True)
    second = jnp.mean(grad_in * normed, axis=axis, keepdims=True)
    return scale_inv * (grad_in - first - normed * second)


def on_device(pair_rep, residue_mask, w_proj, w_gate, w_out, cotangent):
    row_count, columns, channels = pair_rep.shape
    hidden_width = w_out.shape[0]
    row_start = lax.axis_index("dap") * row_count
    col_start = lax.axis_index("ch") * columns
    live_flags = residue_mask.astype(jnp.float32)
    row_live = lax.dynamic_slice_in_dim(live_flags, row_start, row_count, 0)
    col_live = lax.dynamic_slice_in_dim(live_flags, col_start, columns, 0)
    cell_mask = row_live[:, None] * col_live[None, :]
    normed, pair_scale = normalize(pair_rep.astype(jnp.float32), 2)
    normed_half = normed.astype(jnp.bfloat16)
    projected = jnp.einsum("rkd,de->erk", normed_half, w_proj, preferred_element_type=jnp.float32)
    left_sig = jax.nn.sigmoid(projected[:hidden_width])
    left_val = projected[hidden_width : 2 * hidden_width]
    right_sig = jax.nn.sigmoid(projected[2 * hidden_width : 3 * hidden_width])
    right_val = projected[3 * hidden_width :]
    left_cells = (left_sig * left_val * cell_mask).astype(jnp.bfloat16)
    right_cells = (right_sig * right_val * cell_mask).astype(jnp.bfloat16)
    gate_values = jax.nn.sigmoid(
        jnp.einsum("rkd,de->rke", normed_half, w_gate, preferred_element_type=jnp.float32)
    )
    left_rows, right_rows = (
        lax.all_to_all(left_cells, "ch", split_axis=0, concat_axis=2, tiled=True),
        lax.all_to_all(right_cells, "ch", split_axis=0, concat_axis=2, tiled=True),
    )
    product = jnp.einsum(
        "cik,cjk->cij",
        left_rows,
        lax.all_gather(right_rows, "dap", axis=1, tiled=True),
        preferred_element_type=jnp.float32,
    ).astype(jnp.bfloat16)
    product_cells = lax.all_to_all(product, "ch", split_axis=2, concat_axis=0, tiled=True)
    hidden_norm, hidden_scale = normalize(product_cells.astype(jnp.float32), 0)
    hidden_half = hidden_norm.astype(jnp.bfloat16)
    projected_out = jnp.einsum(
        "hrk,hd->rkd", hidden_half, w_out, preferred_element_type=jnp.float32
    )
    pair_update = (gate_values * projected_out).astype(jnp.bfloat16)
    upstream = cotangent.astype(jnp.float32)
    grad_out = (upstream * gate_values).astype(jnp.bfloat16)
    grad_logit = (upstream * projected_out * gate_values * (1.0 - gate_values)).astype(jnp.bfloat16)
    grad_hidden = jnp.einsum("rkd,hd->hrk", grad_out, w_out, preferred_element_type=jnp.float32)
    grad_product = norm_back(grad_hidden, hidden_norm, hidden_scale, 0).astype(jnp.bfloat16)
    grad_rows = lax.all_to_all(grad_product, "ch", split_axis=0, concat_axis=2, tiled=True)
    piece_left = lax.all_gather(left_rows, "dap", axis=1, tiled=True)
    piece_right = lax.all_gather(right_rows, "dap", axis=1, tiled=True)
    piece_grad = lax.all_gather(grad_rows, "dap", axis=1, tiled=True)
    cross_slab = lax.dynamic_slice_in_dim(piece_grad, row_start, row_count, 2)
    new_left = jnp.einsum(
        "cij,cjk->cik", grad_rows, piece_right, preferred_element_type=jnp.float32
    )
    new_right = jnp.einsum(
        "cij,cik->cjk", cross_slab, piece_left, preferred_element_type=jnp.float32
    )
    left_back, right_back = (
        lax.all_to_all(
            new_left.astype(jnp.bfloat16), "ch", split_axis=2, concat_axis=0, tiled=True
        ),
        lax.all_to_all(
            new_right.astype(jnp.bfloat16), "ch", split_axis=2, concat_axis=0, tiled=True
        ),
    )
    masked_left = left_back.astype(jnp.float32) * cell_mask
    masked_right = right_back.astype(jnp.float32) * cell_mask
    grad_proj = jnp.concatenate(
        [
            masked_left * left_val * left_sig * (1.0 - left_sig),
            masked_left * left_sig,
            masked_right * right_val * right_sig * (1.0 - right_sig),
            masked_right * right_sig,
        ],
        axis=0,
    ).astype(jnp.bfloat16)
    grad_normed = jnp.einsum("erk,de->rkd", grad_proj, w_proj, preferred_element_type=jnp.float32)
    grad_normed = grad_normed + jnp.einsum(
        "rke,de->rkd", grad_logit, w_gate, preferred_element_type=jnp.float32
    )
    grad_pair = norm_back(grad_normed, normed, pair_scale, 2).astype(jnp.bfloat16)
    return (pair_update, grad_pair)


def solution(mesh):
    return jax.shard_map(
        on_device,
        mesh=mesh,
        in_specs=(P("dap", "ch", None), P(), P(), P(), P(), P("dap", "ch", None)),
        out_specs=(P("dap", "ch", None), P("dap", "ch", None)),
        check_vma=False,
    )
```

profile of v0, /device:TPU:0, one launch (start us, length us, event | category | flops | bytes accessed | tf_op | source)
XLA Modules:
  0.0 124.0 jit_solution(5858120735575920195)
XLA Ops:
  0.7 1.1 convert_reduce_fusion
  2.1 0.6 copy-done.13
  3.9 1.3 %reshape.95 = bf16[4,2,7200]{2,1,0:T(2,128)(2,1)} reshape(bf16[128,15,30]{2,1,0:T(8,128)(2,1)S(1)} %copy.73) | data formatting | bytes 230400
  5.2 5.2 %all-to-all-start.1 = ((bf16[4,2,7200]{2,1,0:T(2,128)(2,1)}), bf16[4,2,7200]{2,1,0:T(2,128)(2,1)S(1)}, u32[]{:S(2)}, u32[]{:S(2)}) async-start(bf16[4,2,7200]{2,1,0:T(2,128)(2,1)} %reshape.95), calls=%async_computation.1 | async-start | bytes 233472 | tf_op jit(solution)/shard_map/all_to_all | solution.py:45
  10.9 1.3 %reshape.97 = bf16[4,2,7200]{2,1,0:T(2,128)(2,1)} reshape(bf16[128,15,30]{2,1,0:T(8,128)(2,1)S(1)} %copy.71) | data formatting | bytes 230400
  12.2 3.2 %all-to-all-done.1 = bf16[4,2,7200]{2,1,0:T(2,128)(2,1)S(1)} async-done(((bf16[4,2,7200]{2,1,0:T(2,128)(2,1)}), bf16[4,2,7200]{2,1,0:T(2,128)(2,1)S(1)}, u32[]{:S(2)}, u32[]{:S(2)}) %all-to-all-start.1) | async-done | bytes 115232 | tf_op jit(solution)/shard_map/all_to_all | solution.py:45
  15.4 3.3 %all-to-all-start = ((bf16[4,2,7200]{2,1,0:T(2,128)(2,1)}), bf16[4,2,7200]{2,1,0:T(2,128)(2,1)S(1)}, u32[]{:S(2)}, u32[]{:S(2)}) async-start(bf16[4,2,7200]{2,1,0:T(2,128)(2,1)} %reshape.97), calls=%async_computation | async-start | bytes 233472 | tf_op jit(solution)/shard_map/all_to_all | solution.py:44
  20.0 17.0 %all_gather.10 = bf16[32,120,120]{2,0,1:T(8,128)(2,1)S(1)} all-gather(bf16[32,15,120]{2,0,1:T(8,128)(2,1)S(1)} %all_to_all.67), channel_id=1, replica_groups=mesh['dap'=8,'ch'=4] {'dap'}, dimensions={1}, use_global_device_ids=true | all-gather | bytes 1036800 | tf_op jit(solution)/shard_map/all_gather | solution.py:50
  38.2 0.6 convolution_convert_fusion.1
  39.7 8.9 %all_to_all.81 = bf16[4,2,7200]{2,1,0:T(2,128)(2,1)S(1)} all-to-all(bf16[4,2,7200]{2,1,0:T(2,128)(2,1)S(1)} %reshape.99), channel_id=1, replica_groups=mesh['dap'=8,'ch'=4] {'ch'}, dimensions={0} | all-to-all | bytes 230400 | tf_op jit(solution)/shard_map/all_to_all | solution.py:53
  49.2 1.0 copy.78
  50.2 1.3 %reshape.89 = f32[32,15,4,30]{3,2,0,1:T(4,128)S(1)} reshape(bf16[32,15,120]{2,0,1:T(8,128)(2,1)} %copy.78) | data formatting | bytes 345600 | tf_op jit(solution)/shard_map/convert_element_type | solution.py:54
  51.7 1.7 %copy.79 = f32[4,32,15,30]{1,0,3,2:T(4,128)} copy(f32[4,32,15,30]{3,0,1,2:T(4,128)S(1)} %bitcast.66) | data formatting | bytes 460800 | tf_op jit(solution)/shard_map/convert_element_type | solution.py:54
  53.5 1.6 %reshape.85 = f32[128,15,30]{0,2,1:T(8,128)S(1)} reshape(f32[4,32,15,30]{1,0,3,2:T(4,128)} %copy.79) | data formatting | bytes 460800 | tf_op jit(solution)/shard_map/convert_element_type | solution.py:54
  56.6 1.0 multiply_convert_fusion.5
  59.1 1.3 %reshape.101 = bf16[4,2,7200]{2,1,0:T(2,128)(2,1)} reshape(bf16[128,15,30]{2,1,0:T(8,128)(2,1)S(1)} %copy.80) | data formatting | bytes 230400
  60.4 3.4 %all-to-all-start.3 = ((bf16[4,2,7200]{2,1,0:T(2,128)(2,1)}), bf16[4,2,7200]{2,1,0:T(2,128)(2,1)S(1)}, u32[]{:S(2)}, u32[]{:S(2)}) async-start(bf16[4,2,7200]{2,1,0:T(2,128)(2,1)} %reshape.101), calls=%async_computation.3 | async-start | bytes 233472 | tf_op jit(solution)/shard_map/all_to_all | solution.py:65
  63.8 16.8 %all_gather.12 = bf16[32,120,120]{2,0,1:T(8,128)(2,1)} all-gather(bf16[32,15,120]{2,0,1:T(8,128)(2,1)S(1)} %copy-done.3), channel_id=1, replica_groups=mesh['dap'=8,'ch'=4] {'dap'}, dimensions={1}, use_global_device_ids=true | all-gather | bytes 1036800 | tf_op jit(solution)/shard_map/all_gather | solution.py:66
  81.9 0.6 convolution_convert_fusion
  82.4 16.5 %all_gather.11 = bf16[32,120,120]{2,0,1:T(8,128)(2,1)S(1)} all-gather(bf16[32,15,120]{2,0,1:T(8,128)(2,1)S(1)} %all_to_all.72), channel_id=1, replica_groups=mesh['dap'=8,'ch'=4] {'dap'}, dimensions={1}, use_global_device_ids=true | all-gather | bytes 1036800 | tf_op jit(solution)/shard_map/all_gather | solution.py:68
  99.4 1.1 reshape.105
  100.5 4.2 %all-to-all-start.4 = ((bf16[4,2,7200]{2,1,0:T(2,128)(2,1)}), bf16[4,2,7200]{2,1,0:T(2,128)(2,1)S(1)}, u32[]{:S(2)}, u32[]{:S(2)}) async-start(bf16[4,2,7200]{2,1,0:T(2,128)(2,1)} %reshape.105), calls=%async_computation.4 | async-start | bytes 233472 | tf_op jit(solution)/shard_map/all_to_all | solution.py:77
  105.0 0.9 copy-done.8
  105.9 0.7 convolution_convert_fusion.2
  107.0 1.1 reshape.103
  108.1 1.5 %all-to-all-done.4 = bf16[4,2,7200]{2,1,0:T(2,128)(2,1)S(1)} async-done(((bf16[4,2,7200]{2,1,0:T(2,128)(2,1)}), bf16[4,2,7200]{2,1,0:T(2,128)(2,1)S(1)}, u32[]{:S(2)}, u32[]{:S(2)}) %all-to-all-start.4) | async-done | bytes 115232 | tf_op jit(solution)/shard_map/all_to_all | solution.py:77
  109.7 3.5 %all-to-all-start.5 = ((bf16[4,2,7200]{2,1,0:T(2,128)(2,1)}), bf16[4,2,7200]{2,1,0:T(2,128)(2,1)S(1)}, u32[]{:S(2)}, u32[]{:S(2)}) async-start(bf16[4,2,7200]{2,1,0:T(2,128)(2,1)} %reshape.103), calls=%async_computation.5 | async-start | bytes 233472 | tf_op jit(solution)/shard_map/all_to_all | solution.py:80
  114.5 1.5 %copy.86 = f32[4,32,15,30]{1,0,3,2:T(4,128)S(1)} copy(f32[4,32,15,30]{3,0,1,2:T(4,128)S(1)} %bitcast.67) | data formatting | bytes 460800 | tf_op jit(solution)/shard_map/convert_element_type | solution.py:84
  116.5 1.5 %all-to-all-done.5 = bf16[4,2,7200]{2,1,0:T(2,128)(2,1)S(1)} async-done(((bf16[4,2,7200]{2,1,0:T(2,128)(2,1)}), bf16[4,2,7200]{2,1,0:T(2,128)(2,1)S(1)}, u32[]{:S(2)}, u32[]{:S(2)}) %all-to-all-start.5) | async-done | bytes 115232 | tf_op jit(solution)/shard_map/all_to_all | solution.py:80
  119.3 1.5 %copy.91 = f32[4,32,15,30]{1,0,3,2:T(4,128)S(1)} copy(f32[4,32,15,30]{3,0,1,2:T(4,128)S(1)} %bitcast.68) | data formatting | bytes 460800 | tf_op jit(solution)/shard_map/convert_element_type | solution.py:85
  121.8 0.6 copy-done.5
  123.0 1.0 fusion.23
  (75 shorter events, 16.0 us)
Async XLA Ops:
  0.6 2.2 %copy-start = (bf16[128,512]{1,0:T(8,128)(2,1)S(1)}, bf16[128,512]{1,0:T(8,128)(2,1)}, u32[]{:S(2)}) copy-start(bf16[128,512]{1,0:T(8,128)(2,1)} %param.8) | copy-start | bytes 393220
  0.6 1.1 copy-start.1
  2.0 0.7 copy-start.13
  5.2 10.2 %all-to-all-start.1 = ((bf16[4,2,7200]{2,1,0:T(2,128)(2,1)}), bf16[4,2,7200]{2,1,0:T(2,128)(2,1)S(1)}, u32[]{:S(2)}, u32[]{:S(2)}) async-start(bf16[4,2,7200]{2,1,0:T(2,128)(2,1)} %reshape.95), calls=%async_computation.1 | async-start | bytes 233472 | tf_op jit(solution)/shard_map/all_to_all | solution.py:45
  15.4 21.6 %all-to-all-start = ((bf16[4,2,7200]{2,1,0:T(2,128)(2,1)}), bf16[4,2,7200]{2,1,0:T(2,128)(2,1)S(1)}, u32[]{:S(2)}, u32[]{:S(2)}) async-start(bf16[4,2,7200]{2,1,0:T(2,128)(2,1)} %reshape.97), calls=%async_computation | async-start | bytes 233472 | tf_op jit(solution)/shard_map/all_to_all | solution.py:44
  38.2 0.6 copy-start.2
  55.1 0.8 copy-start.11
  55.8 0.8 copy-start.12
  56.6 1.0 copy-start.6
  56.6 1.0 copy-start.9
  57.6 0.7 copy-start.4
  60.4 3.5 %copy-start.3 = (bf16[32,15,120]{2,0,1:T(8,128)(2,1)S(1)}, bf16[32,15,120]{2,0,1:T(8,128)(2,1)}, u32[]{:S(2)}) copy-start(bf16[32,15,120]{2,0,1:T(8,128)(2,1)} %copy-done.2) | copy-start | bytes 345604
  60.4 20.2 %all-to-all-start.3 = ((bf16[4,2,7200]{2,1,0:T(2,128)(2,1)}), bf16[4,2,7200]{2,1,0:T(2,128)(2,1)S(1)}, u32[]{:S(2)}, u32[]{:S(2)}) async-start(bf16[4,2,7200]{2,1,0:T(2,128)(2,1)} %reshape.101), calls=%async_computation.3 | async-start | bytes 233472 | tf_op jit(solution)/shard_map/all_to_all | solution.py:65
  100.5 9.2 %all-to-all-start.4 = ((bf16[4,2,7200]{2,1,0:T(2,128)(2,1)}), bf16[4,2,7200]{2,1,0:T(2,128)(2,1)S(1)}, u32[]{:S(2)}, u32[]{:S(2)}) async-start(bf16[4,2,7200]{2,1,0:T(2,128)(2,1)} %reshape.105), calls=%async_computation.4 | async-start | bytes 233472 | tf_op jit(solution)/shard_map/all_to_all | solution.py:77
  104.7 1.2 copy-start.8
  109.7 8.3 %all-to-all-start.5 = ((bf16[4,2,7200]{2,1,0:T(2,128)(2,1)}), bf16[4,2,7200]{2,1,0:T(2,128)(2,1)S(1)}, u32[]{:S(2)}, u32[]{:S(2)}) async-start(bf16[4,2,7200]{2,1,0:T(2,128)(2,1)} %reshape.103), calls=%async_computation.5 | async-start | bytes 233472 | tf_op jit(solution)/shard_map/all_to_all | solution.py:80
  121.5 0.9 copy-start.5
  121.5 1.1 copy-start.7
  121.5 1.1 copy-start.10
where the time goes:
time: 125 us; the launch traced here: 124 us
  blocking collectives  59.2 us (47%)
  local copies, waits for them, and re-layouts  29.6 us (24%)
  starting transfers between devices  19.7 us (16%)
  waiting for transfers between devices  6.2 us (5%)
  matrix products  4.56 us (4%)
  other arithmetic  3.66 us (3%)
    all_gather x1, blocking collectives, on_device(): lax.all_gather(right_rows, 'dap', axis=1, tiled=True)  17 us
    all_gather x1, blocking collectives, on_device(): piece_left = lax.all_gather(left_rows, 'dap', axis=1, tiled=True)  16.8 us
    all_gather x1, blocking collectives, on_device(): piece_grad = lax.all_gather(grad_rows, 'dap', axis=1, tiled=True)  16.5 us
    unnamed x40, local copies, waits for them, and re-layouts  13.1 us
    all_to_all x1, blocking collectives, on_device(): lax.all_to_all(product, 'ch', split_axis=2, concat_axis=0, tiled=True)  8.94 us
    all_to_all x1, starting transfers between devices, on_device(): lax.all_to_all(right_cells, 'ch', split_axis=0, concat_axis=2, tiled=True)  5.19 us
    convert_element_type x3, local copies, waits for them, and re-layouts, on_device(): hidden_norm, hidden_scale = normalize(product_cells.astype(jnp.float32), 0)  4.68 us
    all_to_all x1, starting transfers between devices, on_device(): lax.all_to_all(new_left.astype(jnp.bfloat16), 'ch', split_axis=2, concat_...  4.21 us
  transfers between devices with their start and end apart: 5, of which 3 were waited for; matrix products, arithmetic and copies ran while one was open for 7% of the time, Pallas kernels for 0%

commit v1 on v0

--- a/solution.py
+++ b/solution.py
@@ -50,7 +50,15 @@
         lax.all_gather(right_rows, "dap", axis=1, tiled=True),
         preferred_element_type=jnp.float32,
     ).astype(jnp.bfloat16)
-    product_cells = lax.all_to_all(product, "ch", split_axis=2, concat_axis=0, tiled=True)
+    product_cells = jnp.concatenate(
+        lax.all_to_all(
+            jnp.stack(jnp.split(product, lax.psum(1, axis_name="ch"), 2), 0),
+            axis_name="ch",
+            split_axis=0,
+            concat_axis=0,
+        ),
+        0,
+    )
     hidden_norm, hidden_scale = normalize(product_cells.astype(jnp.float32), 0)
     hidden_half = hidden_norm.astype(jnp.bfloat16)
     projected_out = jnp.einsum(

time: 125 us -> 124 us (level)
  local copies, waits for them, and re-layouts: 29.6 us -> 28.2 us
    convert_element_type x3 -> x2, local copies, waits for them, and re-layouts: 4.68 us -> 3.01 us  [on_device(): hidden_norm, hidden_scale = normalize(product_cells.astype(jnp.float32), 0)]
    unnamed x40 -> x36, local copies, waits for them, and re-layouts: 13.1 us -> 14.6 us
where the time goes in v1:
time: 124 us; the launch traced here: 123 us
  blocking collectives  59.4 us (48%)
  local copies, waits for them, and re-layouts  28.2 us (23%)
  starting transfers between devices  20 us (16%)
  waiting for transfers between devices  6.49 us (5%)
  matrix products  4.57 us (4%)
  other arithmetic  3.63 us (3%)
    all_gather x1, blocking collectives, on_device(): lax.all_gather(right_rows, 'dap', axis=1, tiled=True)  17 us
    all_gather x1, blocking collectives, on_device(): piece_left = lax.all_gather(left_rows, 'dap', axis=1, tiled=True)  16.9 us
    all_gather x1, blocking collectives, on_device(): piece_grad = lax.all_gather(grad_rows, 'dap', axis=1, tiled=True)  16.5 us
    unnamed x36, local copies, waits for them, and re-layouts  14.6 us
    all_to_all x1, blocking collectives, on_device(): lax.all_to_all(jnp.stack(jnp.split(product, lax.psum(1, axis_name='ch'),...  8.94 us
    all_to_all x1, starting transfers between devices, on_device(): lax.all_to_all(right_cells, 'ch', split_axis=0, concat_axis=2, tiled=True)  5.19 us
    all_to_all x1, starting transfers between devices, on_device(): lax.all_to_all(new_left.astype(jnp.bfloat16), 'ch', split_axis=2, concat_...  4.22 us
    all_to_all x1, starting transfers between devices, on_device(): lax.all_to_all(new_right.astype(jnp.bfloat16), 'ch', split_axis=2, concat...  3.93 us
  transfers between devices with their start and end apart: 5, of which 3 were waited for; matrix products, arithmetic and copies ran while one was open for 7% of the time, Pallas kernels for 0%

profile of v1, /device:TPU:0, one launch (start us, length us, event | category | flops | bytes accessed | tf_op | source)
XLA Modules:
  0.0 123.3 jit_solution(1814286337090860428)
XLA Ops:
  0.7 1.1 convert_reduce_fusion.1
  2.1 0.6 copy-done.11
  3.9 1.3 %reshape.90 = bf16[4,2,7200]{2,1,0:T(2,128)(2,1)} reshape(bf16[128,15,30]{2,1,0:T(8,128)(2,1)S(1)} %copy.70) | data formatting | bytes 230400
  5.2 5.2 %all-to-all-start.1 = ((bf16[4,2,7200]{2,1,0:T(2,128)(2,1)}), bf16[4,2,7200]{2,1,0:T(2,128)(2,1)S(1)}, u32[]{:S(2)}, u32[]{:S(2)}) async-start(bf16[4,2,7200]{2,1,0:T(2,128)(2,1)} %reshape.90), calls=%async_computation.1 | async-start | bytes 233472 | tf_op jit(solution)/shard_map/all_to_all | solution.py:45
  10.9 1.3 %reshape.92 = bf16[4,2,7200]{2,1,0:T(2,128)(2,1)} reshape(bf16[128,15,30]{2,1,0:T(8,128)(2,1)S(1)} %copy.68) | data formatting | bytes 230400
  12.2 3.2 %all-to-all-done.1 = bf16[4,2,7200]{2,1,0:T(2,128)(2,1)S(1)} async-done(((bf16[4,2,7200]{2,1,0:T(2,128)(2,1)}), bf16[4,2,7200]{2,1,0:T(2,128)(2,1)S(1)}, u32[]{:S(2)}, u32[]{:S(2)}) %all-to-all-start.1) | async-done | bytes 115232 | tf_op jit(solution)/shard_map/all_to_all | solution.py:45
  15.4 3.3 %all-to-all-start = ((bf16[4,2,7200]{2,1,0:T(2,128)(2,1)}), bf16[4,2,7200]{2,1,0:T(2,128)(2,1)S(1)}, u32[]{:S(2)}, u32[]{:S(2)}) async-start(bf16[4,2,7200]{2,1,0:T(2,128)(2,1)} %reshape.92), calls=%async_computation | async-start | bytes 233472 | tf_op jit(solution)/shard_map/all_to_all | solution.py:44
  20.0 17.0 %all_gather.10 = bf16[32,120,120]{2,0,1:T(8,128)(2,1)S(1)} all-gather(bf16[32,15,120]{2,0,1:T(8,128)(2,1)S(1)} %all_to_all.63), channel_id=1, replica_groups=mesh['dap'=8,'ch'=4] {'dap'}, dimensions={1}, use_global_device_ids=true | all-gather | bytes 1036800 | tf_op jit(solution)/shard_map/all_gather | solution.py:50
  38.2 0.6 convolution_convert_fusion.1
  39.3 0.6 reshape.94
  39.9 8.9 %all_to_all.77 = bf16[4,2,7200]{2,1,0:T(2,128)(2,1)S(1)} all-to-all(bf16[4,2,7200]{2,1,0:T(2,128)(2,1)S(1)} %reshape.94), channel_id=1, replica_groups=mesh['dap'=8,'ch'=4] {'ch'}, dimensions={0} | all-to-all | bytes 230400 | tf_op jit(solution)/shard_map/all_to_all | solution.py:54
  48.9 0.8 reshape.95
  49.8 1.4 %copy.75 = f32[4,32,15,30]{1,0,3,2:T(4,128)} copy(bf16[4,32,15,30]{3,1,2,0:T(8,128)(2,1)S(1)} %bitcast.73) | data formatting | bytes 345600 | tf_op jit(solution)/shard_map/convert_element_type | solution.py:62
  51.2 1.6 %reshape.82 = f32[128,15,30]{0,2,1:T(8,128)S(1)} reshape(f32[4,32,15,30]{1,0,3,2:T(4,128)} %copy.75) | data formatting | bytes 460800 | tf_op jit(solution)/shard_map/convert_element_type | solution.py:62
  54.3 1.0 multiply_convert_fusion.5
  56.8 1.3 %reshape.96 = bf16[4,2,7200]{2,1,0:T(2,128)(2,1)} reshape(bf16[128,15,30]{2,1,0:T(8,128)(2,1)S(1)} %copy.76) | data formatting | bytes 230400
  58.1 3.3 %all-to-all-start.3 = ((bf16[4,2,7200]{2,1,0:T(2,128)(2,1)}), bf16[4,2,7200]{2,1,0:T(2,128)(2,1)S(1)}, u32[]{:S(2)}, u32[]{:S(2)}) async-start(bf16[4,2,7200]{2,1,0:T(2,128)(2,1)} %reshape.96), calls=%async_computation.3 | async-start | bytes 233472 | tf_op jit(solution)/shard_map/all_to_all | solution.py:73
  61.4 16.9 %all_gather.12 = bf16[32,120,120]{2,0,1:T(8,128)(2,1)} all-gather(bf16[32,15,120]{2,0,1:T(8,128)(2,1)S(1)} %all_to_all.59), channel_id=1, replica_groups=mesh['dap'=8,'ch'=4] {'dap'}, dimensions={1}, use_global_device_ids=true | all-gather | bytes 1036800 | tf_op jit(solution)/shard_map/all_gather | solution.py:74
  80.2 16.5 %all_gather.11 = bf16[32,120,120]{2,0,1:T(8,128)(2,1)S(1)} all-gather(bf16[32,15,120]{2,0,1:T(8,128)(2,1)S(1)} %all_to_all.68), channel_id=1, replica_groups=mesh['dap'=8,'ch'=4] {'dap'}, dimensions={1}, use_global_device_ids=true | all-gather | bytes 1036800 | tf_op jit(solution)/shard_map/all_gather | solution.py:76
  97.1 1.1 reshape.100
  98.2 4.2 %all-to-all-start.4 = ((bf16[4,2,7200]{2,1,0:T(2,128)(2,1)}), bf16[4,2,7200]{2,1,0:T(2,128)(2,1)S(1)}, u32[]{:S(2)}, u32[]{:S(2)}) async-start(bf16[4,2,7200]{2,1,0:T(2,128)(2,1)} %reshape.100), calls=%async_computation.4 | async-start | bytes 233472 | tf_op jit(solution)/shard_map/all_to_all | solution.py:85
  102.8 0.9 copy-done.6
  103.6 0.7 convolution_convert_fusion.2
  104.8 1.1 reshape.98
  105.9 1.5 %all-to-all-done.4 = bf16[4,2,7200]{2,1,0:T(2,128)(2,1)S(1)} async-done(((bf16[4,2,7200]{2,1,0:T(2,128)(2,1)}), bf16[4,2,7200]{2,1,0:T(2,128)(2,1)S(1)}, u32[]{:S(2)}, u32[]{:S(2)}) %all-to-all-start.4) | async-done | bytes 115232 | tf_op jit(solution)/shard_map/all_to_all | solution.py:85
  107.4 3.9 %all-to-all-start.5 = ((bf16[4,2,7200]{2,1,0:T(2,128)(2,1)}), bf16[4,2,7200]{2,1,0:T(2,128)(2,1)}, u32[]{:S(2)}, u32[]{:S(2)}) async-start(bf16[4,2,7200]{2,1,0:T(2,128)(2,1)} %reshape.98), calls=%async_computation.5 | async-start | bytes 233472 | tf_op jit(solution)/shard_map/all_to_all | solution.py:88
  112.7 1.5 %copy.82 = f32[4,32,15,30]{1,0,3,2:T(4,128)S(1)} copy(f32[4,32,15,30]{3,0,1,2:T(4,128)S(1)} %bitcast.74) | data formatting | bytes 460800 | tf_op jit(solution)/shard_map/convert_element_type | solution.py:92
  114.6 1.8 %all-to-all-done.5 = bf16[4,2,7200]{2,1,0:T(2,128)(2,1)} async-done(((bf16[4,2,7200]{2,1,0:T(2,128)(2,1)}), bf16[4,2,7200]{2,1,0:T(2,128)(2,1)}, u32[]{:S(2)}, u32[]{:S(2)}) %all-to-all-start.5) | async-done | bytes 115232 | tf_op jit(solution)/shard_map/all_to_all | solution.py:88
  116.4 1.4 %reshape.99 = bf16[120,15,32]{2,1,0:T(8,128)(2,1)S(1)} reshape(bf16[4,2,7200]{2,1,0:T(2,128)(2,1)} %all-to-all-done.5) | data formatting | bytes 230400
  118.6 1.5 %copy.87 = f32[4,32,15,30]{1,0,3,2:T(4,128)S(1)} copy(f32[4,32,15,30]{3,0,1,2:T(4,128)S(1)} %bitcast.75) | data formatting | bytes 460800 | tf_op jit(solution)/shard_map/convert_element_type | solution.py:93
  121.2 0.6 copy-done.3
  122.3 1.0 fusion.23
  (71 shorter events, 15.1 us)
Async XLA Ops:
  0.6 2.2 %copy-start = (bf16[128,512]{1,0:T(8,128)(2,1)S(1)}, bf16[128,512]{1,0:T(8,128)(2,1)}, u32[]{:S(2)}) copy-start(bf16[128,512]{1,0:T(8,128)(2,1)} %param.8) | copy-start | bytes 393220
  0.6 1.1 copy-start.1
  2.0 0.7 copy-start.11
  5.2 10.2 %all-to-all-start.1 = ((bf16[4,2,7200]{2,1,0:T(2,128)(2,1)}), bf16[4,2,7200]{2,1,0:T(2,128)(2,1)S(1)}, u32[]{:S(2)}, u32[]{:S(2)}) async-start(bf16[4,2,7200]{2,1,0:T(2,128)(2,1)} %reshape.90), calls=%async_computation.1 | async-start | bytes 233472 | tf_op jit(solution)/shard_map/all_to_all | solution.py:45
  15.4 21.6 %all-to-all-start = ((bf16[4,2,7200]{2,1,0:T(2,128)(2,1)}), bf16[4,2,7200]{2,1,0:T(2,128)(2,1)S(1)}, u32[]{:S(2)}, u32[]{:S(2)}) async-start(bf16[4,2,7200]{2,1,0:T(2,128)(2,1)} %reshape.92), calls=%async_computation | async-start | bytes 233472 | tf_op jit(solution)/shard_map/all_to_all | solution.py:44
  52.8 0.8 copy-start.8
  53.5 0.8 copy-start.9
  54.3 1.0 copy-start.4
  54.3 1.0 copy-start.7
  55.3 0.7 copy-start.2
  58.1 20.3 %all-to-all-start.3 = ((bf16[4,2,7200]{2,1,0:T(2,128)(2,1)}), bf16[4,2,7200]{2,1,0:T(2,128)(2,1)S(1)}, u32[]{:S(2)}, u32[]{:S(2)}) async-start(bf16[4,2,7200]{2,1,0:T(2,128)(2,1)} %reshape.96), calls=%async_computation.3 | async-start | bytes 233472 | tf_op jit(solution)/shard_map/all_to_all | solution.py:73
  98.2 9.2 %all-to-all-start.4 = ((bf16[4,2,7200]{2,1,0:T(2,128)(2,1)}), bf16[4,2,7200]{2,1,0:T(2,128)(2,1)S(1)}, u32[]{:S(2)}, u32[]{:S(2)}) async-start(bf16[4,2,7200]{2,1,0:T(2,128)(2,1)} %reshape.100), calls=%async_computation.4 | async-start | bytes 233472 | tf_op jit(solution)/shard_map/all_to_all | solution.py:85
  102.4 1.2 copy-start.6
  107.4 9.0 %all-to-all-start.5 = ((bf16[4,2,7200]{2,1,0:T(2,128)(2,1)}), bf16[4,2,7200]{2,1,0:T(2,128)(2,1)}, u32[]{:S(2)}, u32[]{:S(2)}) async-start(bf16[4,2,7200]{2,1,0:T(2,128)(2,1)} %reshape.98), calls=%async_computation.5 | async-start | bytes 233472 | tf_op jit(solution)/shard_map/all_to_all | solution.py:88
  120.8 0.9 copy-start.3
  120.8 1.1 copy-start.5
  120.9 1.0 copy-start.10
